TPU v7x, 256 devices: a whole 4x4x8 slice. The times are simulated.
256 devices in a mesh: space: 32 (over y_hi, z, core), coil: 8 (over y_lo, x).
Axes of the slice: x: 4, y: 4 (y_hi: 2, y_lo: 2; y = y_hi * 2 + y_lo), z: 8, core: 2. Of those that a mesh axis runs over, the one named last changes fastest.
Arguments:
- spatial_coef: bfloat16 [16, 128, 128, 2, 128], P('coil', 'space'), may hold values from -6 to 6
- temporal_basis: bfloat16 [2, 16, 4], replicated, may hold values from -1.5 to 1.5
- coil_maps: bfloat16 [32, 128, 128, 2, 128], P('coil', 'space'), may hold values from -6 to 6
- field_steps: int32 [128, 128, 128], P('space'), may hold values from 0 to 255
- kspace_data: bfloat16 [32, 4, 128, 128, 2, 128], P('coil', None, None, 'space'), may hold values from -6 to 6
- sample_mask: int32 [4, 128, 128], P(None, 'space'), may hold values 0 or 1
Outputs:
- gradient: float32 [16, 128, 128, 2, 128], P('coil', 'space')
Inputs may be any that keep to these rules, and one draw needn't show every extreme that they name: `sample_mask`: 1 where a phase-encoding line is sampled at that point, else 0.
All inputs are finite; a program needn't handle non-finite values. No bound on the sum of `sample_mask` on one device may be relied on, other than what follows from the above.
Results may differ from a plain program's by a relative error of at most 0.014.
Values may be sent and summed in bfloat16 or wider, within the bound.
A program may use at most 64 MiB of HBM per device.

v0:
```python
import math
import jax
import jax.numpy as jnp
from jax import lax
from jax.sharding import PartitionSpec as P

STEPS_CYCLE = 256


def dft_table(length, sign):
    index = jnp.arange(length, dtype=jnp.int32)
    steps = index[:, None] * index[None, :] % length
    angle = steps.astype(jnp.float32) * (2.0 * math.pi / length)
    scale = 1.0 / math.sqrt(length)
    cosine = jnp.cos(angle) * scale
    sine = jnp.sin(angle) * (sign * scale)
    upper = jnp.stack([cosine, sine], axis=1)
    lower = jnp.stack([-sine, cosine], axis=1)
    return jnp.stack([upper, lower], axis=0).astype(jnp.bfloat16)


def forward_mix(basis):
    real_part = basis[0]
    imaginary = basis[1]
    return jnp.stack(
        [jnp.stack([real_part, imaginary], -1), jnp.stack([-imaginary, real_part], -1)], 1
    )


def adjoint_mix(basis):
    real_part = basis[0].T
    imaginary = basis[1].T
    return jnp.stack(
        [jnp.stack([real_part, -imaginary], -1), jnp.stack([imaginary, real_part], -1)], 1
    )


def phase_parts(field_steps, points):
    counter = jnp.arange(1, points + 1, dtype=jnp.int32)
    steps = field_steps[None] * counter[:, None, None, None] % STEPS_CYCLE
    angle = steps.astype(jnp.float32) * (2.0 * math.pi / STEPS_CYCLE)
    return (jnp.cos(angle), jnp.sin(angle))


def transform(volume, table, form):
    return jnp.einsum(form, volume, table, preferred_element_type=jnp.float32)


def shards(spatial_coef, temporal_basis, coil_maps, field_steps, kspace_data, sample_mask):
    points = temporal_basis.shape[2]
    section = temporal_basis
    image = jnp.einsum(
        "lxypz,lptq->txyqz",
        lax.all_gather(spatial_coef, "coil", axis=0, tiled=True),
        forward_mix(section),
        preferred_element_type=jnp.float32,
    )
    cosine, sine = phase_parts(field_steps, points)
    image_real = image[:, :, :, 0]
    image_imaginary = image[:, :, :, 1]
    turned_real = cosine * image_real - sine * image_imaginary
    turned_imaginary = sine * image_real + cosine * image_imaginary
    map_real = coil_maps[:, :, :, 0].astype(jnp.float32)[:, None]
    map_imaginary = coil_maps[:, :, :, 1].astype(jnp.float32)[:, None]
    coil_real = map_real * turned_real - map_imaginary * turned_imaginary
    coil_imaginary = map_real * turned_imaginary + map_imaginary * turned_real
    coil_image = jnp.stack([coil_real, coil_imaginary], axis=4).astype(jnp.bfloat16)
    depth_count = coil_image.shape[5]
    row_count = coil_image.shape[3]
    depth_pass = transform(coil_image, dft_table(depth_count, -1.0), "ctxypz,pzqk->ctxyqk").astype(
        jnp.bfloat16
    )
    row_pass = transform(depth_pass, dft_table(row_count, -1.0), "ctxypz,pyqk->ctxkqz").astype(
        jnp.bfloat16
    )
    slabs = lax.all_to_all(row_pass, "space", split_axis=3, concat_axis=2, tiled=True)
    first_count = slabs.shape[2]
    kspace = transform(slabs, dft_table(first_count, -1.0), "ctxypz,pxqk->ctkyqz")
    mask_float = sample_mask.astype(jnp.float32)[None, :, None, :, None, :]
    residual = (mask_float * (kspace - kspace_data.astype(jnp.float32))).astype(jnp.bfloat16)
    back_first = transform(residual, dft_table(first_count, 1.0), "ctxypz,pxqk->ctkyqz").astype(
        jnp.bfloat16
    )
    returned = lax.all_to_all(back_first, "space", split_axis=2, concat_axis=3, tiled=True)
    back_rows = transform(returned, dft_table(row_count, 1.0), "ctxypz,pyqk->ctxkqz").astype(
        jnp.bfloat16
    )
    back_image = transform(back_rows, dft_table(depth_count, 1.0), "ctxypz,pzqk->ctxyqk")
    back_real = back_image[:, :, :, :, 0]
    back_imaginary = back_image[:, :, :, :, 1]
    sum_real = jnp.sum(map_real * back_real + map_imaginary * back_imaginary, axis=0)
    sum_imaginary = jnp.sum(map_real * back_imaginary - map_imaginary * back_real, axis=0)
    combined_real = cosine * sum_real + sine * sum_imaginary
    combined_imaginary = cosine * sum_imaginary - sine * sum_real
    combined = jnp.stack([combined_real, combined_imaginary], axis=3)
    section = temporal_basis.astype(jnp.float32)
    return lax.psum_scatter(
        jnp.einsum(
            "txypz,tplq->lxyqz", combined, adjoint_mix(section), precision=lax.Precision.HIGHEST
        ).astype(jnp.bfloat16),
        "coil",
        scatter_dimension=0,
        tiled=True,
    ).astype(jnp.float32)


def solution(mesh):
    in_specs = (
        P("coil", "space", None, None, None),
        P(),
        P("coil", "space", None, None, None),
        P("space", None, None),
        P("coil", None, None, "space", None, None),
        P(None, "space", None),
    )
    out_specs = P("coil", "space", None, None, None)
    return jax.shard_map(shards, mesh=mesh, in_specs=in_specs, out_specs=out_specs, check_vma=False)
```

profile of v0, /device:TPU:1, one launch (start us, length us, event | category | flops | bytes accessed | tf_op | source)
XLA Modules:
  0.0 418.4 jit_solution(10272380356210166558)
XLA Ops:
  6.5 0.0 all-gather.2.cloned.1.call-start
  6.5 1.9 copy.65
  8.5 0.0 all-gather.2.cloned.1.call-update
  8.5 0.7 fusion.72
  9.2 0.7 slice_bitcast_fusion.6
  9.9 0.3 multiply_convert_fusion.2
  10.2 0.3 negate_convert_fusion
  10.5 0.3 multiply_convert_fusion
  10.8 3.6 slice_convert_fusion.1
  14.4 53.7 %all-gather.2.cloned.1.call-done = bf16[16,4,128,2,128]{4,2,3,1,0:T(8,128)(2,1)} async-done(((bf16[2,4,128,2,128]{4,2,3,1,0:T(8,128)(2,1)}), bf16[16,4,128,2,128]{4,2,3,1,0:T(8,128)(2,1)}) %all-gather.2.cloned.1.call-update) | async-done | bytes 4194320 | tf_op jit(solution)/shard_map/all_gather | solution.py:54
  68.1 0.0 copy-start.1
  68.1 4.9 %fusion.31 = f32[4,2,4,128,128]{4,0,3,2,1:T(4,128)S(1)} fusion(bf16[16,4,128,2,128]{4,2,3,1,0:T(8,128)(2,1)} %all-gather.2.cloned.1.call-done, bf16[16,1,4,2]{0,2,1,3:T(4,128)(2,1)S(1)} %get-tuple-element.26, bf16[16,1,4,2]{0,2,1,3:T(4,128)(2,1)S(1)} %get-tuple-element.25), kind=kOutput, calls=%fused_computation.43 | convolution fusion | flops 33555456 | bytes 6291968 | tf_op jit(solution)/shard_map/lxypz,lptq->txyqz/dot_general | solution.py:52
  73.0 0.3 copy.134
  73.2 0.0 copy-done.1
  73.2 4.6 %multiply_subtract_fusion = (f32[4,4,128,128]{3,2,1,0:T(8,128)S(1)}, f32[4,4,128,128]{3,2,1,0:T(8,128)S(1)}) fusion(f32[4,4,128,2,128]{4,2,1,0,3:T(8,128)S(1)} %bitcast.244, s32[4]{0:T(128)S(1)} %iota_add_fusion, s32[4,128,128]{2,1,0:T(8,128)S(1)} %copy-done.1), kind=kLoop, calls=%fused_computation.64 | loop fusion | flops 5242880 | bytes 4456464 | tf_op jit(solution)/shard_map/sub | solution.py:61
  77.9 3.1 subtract_convert_fusion
  81.0 6.7 %fusion.5 = bf16[4,4,4,128,2,128]{5,3,2,1,0,4:T(8,128)(2,1)} fusion(bf16[4,4,4,128,1,128]{5,3,4,2,1,0:T(8,128)(2,1)} %get-tuple-element.8, bf16[4,4,4,128,1,128]{5,3,4,2,1,0:T(8,128)(2,1)} %get-tuple-element.7, bf16[1,128,2,128]{3,1,0,2:T(8,128)(2,1)S(1)} %get-tuple-element.16, bf16[1,128,2,128]{3,1,0,2:T(8,128)(2,1)S(1)} %get-tuple-element.17), kind=kOutput, calls=%fused_computation.10 | convolution fusion | flops 2160590848 | bytes 8519680 | tf_op jit(solution)/shard_map/ctxypz,pyqk->ctxkqz/dot_general | solution.py:46
  87.7 7.4 %copy.69 = bf16[4,4,4,128,2,128]{5,2,1,0,4,3:T(4,128)(2,1)} copy(bf16[4,4,4,128,2,128]{5,3,2,1,0,4:T(8,128)(2,1)} %fusion.5) | data formatting | bytes 8388608 | tf_op jit(solution)/shard_map/convert_element_type | solution.py:73
  95.1 0.0 copy-start.3
  95.1 10.2 %all-to-all-start = ((bf16[4,4,4,128,2,128]{5,2,1,0,4,3:T(4,128)(2,1)}), bf16[4,4,4,128,2,128]{5,2,1,0,4,3:T(4,128)(2,1)}, u32[]{:S(2)}, u32[]{:S(2)}) async-start(bf16[4,4,4,128,2,128]{5,2,1,0,4,3:T(4,128)(2,1)} %copy.69), calls=%async_computation | async-start | bytes 8388608 | tf_op jit(solution)/shard_map/all_to_all | solution.py:76
  105.3 0.0 copy-done.3
  105.3 96.1 %all-to-all-done = bf16[4,4,4,128,2,128]{5,2,1,0,4,3:T(4,128)(2,1)} async-done(((bf16[4,4,4,128,2,128]{5,2,1,0,4,3:T(4,128)(2,1)}), bf16[4,4,4,128,2,128]{5,2,1,0,4,3:T(4,128)(2,1)}, u32[]{:S(2)}, u32[]{:S(2)}) %all-to-all-start) | async-done | bytes 4194336 | tf_op jit(solution)/shard_map/all_to_all | solution.py:76
  201.5 0.0 copy-start
  201.5 4.7 %copy.70 = bf16[4,4,4,32,4,2,128]{6,2,3,5,4,1,0:T(4,128)(2,1)S(1)} copy(bf16[4,4,4,32,4,2,128]{6,2,1,0,5,4,3:T(4,128)(2,1)} %bitcast.51) | data formatting | bytes 8388608 | tf_op jit(solution)/shard_map/all_to_all | solution.py:76
  206.2 0.0 copy-done
  206.2 1.4 fusion.1
  207.6 1.3 fusion.6
  208.8 5.2 %copy.75 = bf16[4,4,128,4,2,128]{5,3,1,0,4,2:T(4,128)(2,1)} copy(bf16[4,4,128,4,2,128]{5,2,3,1,0,4:T(8,128)(2,1)S(1)} %fusion.6) | data formatting | bytes 8388608 | tf_op jit(solution)/shard_map/convert_element_type | solution.py:81
  214.1 0.0 copy-start.2
  214.1 7.4 %all-to-all-start.1 = ((bf16[4,4,128,4,2,128]{5,3,1,0,4,2:T(4,128)(2,1)}), bf16[4,4,128,4,2,128]{5,3,1,0,4,2:T(4,128)(2,1)}, u32[]{:S(2)}, u32[]{:S(2)}) async-start(bf16[4,4,128,4,2,128]{5,3,1,0,4,2:T(4,128)(2,1)} %copy.75), calls=%async_computation.1 | async-start | bytes 8388608 | tf_op jit(solution)/shard_map/all_to_all | solution.py:84
  221.5 0.0 reduce-scatter.2.cloned.1.call-start
  221.5 0.0 copy-done.2
  221.6 96.1 %all-to-all-done.1 = bf16[4,4,128,4,2,128]{5,3,1,0,4,2:T(4,128)(2,1)} async-done(((bf16[4,4,128,4,2,128]{5,3,1,0,4,2:T(4,128)(2,1)}), bf16[4,4,128,4,2,128]{5,3,1,0,4,2:T(4,128)(2,1)}, u32[]{:S(2)}, u32[]{:S(2)}) %all-to-all-start.1) | async-done | bytes 4194336 | tf_op jit(solution)/shard_map/all_to_all | solution.py:84
  317.7 6.5 %copy.76 = bf16[4,4,32,4,4,2,128]{6,4,2,5,3,1,0:T(4,128)(2,1)} copy(bf16[4,4,32,4,4,2,128]{6,4,1,0,5,3,2:T(4,128)(2,1)} %bitcast.62) | data formatting | bytes 8388608 | tf_op jit(solution)/shard_map/all_to_all | solution.py:84
  324.2 7.8 %fusion.20 = f32[4,4,4,128,2,128]{5,3,4,2,1,0:T(8,128)} fusion(bf16[4,4,4,128,2,128,1]{5,3,6,4,2,1,0:T(8,128)(2,1)} %bitcast.238, bf16[1,128,2,128]{3,1,2,0:T(8,128)(2,1)S(1)} %get-tuple-element.18, bf16[1,128,2,128]{3,1,2,0:T(8,128)(2,1)S(1)} %get-tuple-element.15), kind=kOutput, calls=%fused_computation.31 | convolution fusion | flops 2150105088 | bytes 12713984 | tf_op jit(solution)/shard_map/ctxypz,pzqk->ctxyqk/dot_general | solution.py:46
  332.0 4.6 %add_reduce_fusion = (f32[4,4,128,128]{3,2,1,0:T(8,128)S(1)}, f32[4,4,128,128]{3,2,1,0:T(8,128)S(1)}) fusion(f32[4,4,4,128,2,128]{5,3,4,2,1,0:T(8,128)} %fusion.20, f32[4,4,128,128]{3,2,1,0:T(8,128)S(1)} %bitcast.243, f32[4,4,128,128]{3,2,1,0:T(8,128)S(1)} %bitcast.241), kind=kLoop, calls=%fused_computation.28 | loop fusion | flops 7864320 | bytes 12582912 | tf_op jit(solution)/shard_map/reduce_sum | solution.py:91
  336.6 9.6 %fusion.40 = (f32[4,4,128,1,128]{4,0,3,2,1:T(4,128)S(1)}, f32[4,4,128,1,128]{4,0,3,2,1:T(4,128)S(1)}) fusion(f32[4,4,128,128]{3,2,1,0:T(8,128)S(1)} %get-tuple-element.6, f32[4,4,128,128]{3,2,1,0:T(8,128)S(1)} %get-tuple-element.5, s32[4]{0:T(128)S(1)} %iota_add_fusion, s32[4,128,128]{2,1,0:T(8,128)S(1)} %copy-done.1), kind=kLoop, calls=%fused_computation.58 | loop fusion | flops 5242880 | bytes 4456464 | tf_op jit(solution)/shard_map/add | solution.py:93
  346.2 7.8 %fusion.7 = bf16[16,4,128,2,128]{4,0,2,1,3:T(8,128)(2,1)S(1)} fusion(f32[4,4,128,1,128]{4,0,3,2,1:T(4,128)S(1)} %get-tuple-element.10, f32[4,4,128,1,128]{4,0,3,2,1:T(4,128)S(1)} %get-tuple-element.9, f32[4,1,16,2]{2,0,1,3:T(4,128)S(1)} %get-tuple-element.22, f32[4,1,16,2]{2,0,1,3:T(4,128)S(1)} %get-tuple-element.21), kind=kOutput, calls=%fused_computation.12 | convolution fusion | flops 203948288 | bytes 6292480 | tf_op jit(solution)/shard_map/txypz,tplq->lxyqz/dot_general | solution.py:98
  354.0 3.1 copy.82
  357.1 0.0 reduce-scatter.2.cloned.1.call-update
  357.1 51.9 %reduce-scatter.2.cloned.1.call-done = bf16[2,4,128,2,128]{4,2,3,1,0:T(8,128)(2,1)} async-done(((bf16[16,4,128,2,128]{4,2,3,1,0:T(8,128)(2,1)}), bf16[2,4,128,2,128]{4,2,3,1,0:T(8,128)(2,1)}) %reduce-scatter.2.cloned.1.call-update) | async-done | bytes 524304 | tf_op jit(solution)/shard_map/reduce_scatter | solution.py:97
  409.0 2.6 copy.83
  (8 shorter events, 0.1 us)
Async XLA Ops:
  6.5 61.6 %all-gather.2.cloned.1.call-start = ((), (), s32[]{:S(2)}) async-start(), calls=%async_computation.3 | async-start | bytes 4718592 | tf_op jit(solution)/shard_map/all_gather | solution.py:54
  68.1 5.1 %copy-start.1 = (s32[4,128,128]{2,1,0:T(8,128)S(1)}, s32[4,128,128]{2,1,0:T(8,128)}, u32[]{:S(2)}) copy-start(s32[4,128,128]{2,1,0:T(8,128)} %param.9) | copy-start | bytes 786436
  95.1 10.2 %copy-start.3 = (s32[4,4,128]{2,1,0:T(4,128)S(1)}, s32[4,4,128]{2,1,0:T(4,128)}, u32[]{:S(2)}) copy-start(s32[4,4,128]{2,1,0:T(4,128)} %param.11) | copy-start | bytes 24580
  95.1 106.3 %all-to-all-start = ((bf16[4,4,4,128,2,128]{5,2,1,0,4,3:T(4,128)(2,1)}), bf16[4,4,4,128,2,128]{5,2,1,0,4,3:T(4,128)(2,1)}, u32[]{:S(2)}, u32[]{:S(2)}) async-start(bf16[4,4,4,128,2,128]{5,2,1,0,4,3:T(4,128)(2,1)} %copy.69), calls=%async_computation | async-start | bytes 8388608 | tf_op jit(solution)/shard_map/all_to_all | solution.py:76
  201.5 4.7 %copy-start = (bf16[4,4,128,4,2,128]{5,4,3,2,1,0:T(2,128)(2,1)S(1)}, bf16[4,4,128,4,2,128]{5,4,3,2,1,0:T(2,128)(2,1)}, u32[]{:S(2)}) copy-start(bf16[4,4,128,4,2,128]{5,4,3,2,1,0:T(2,128)(2,1)} %param.10) | copy-start | bytes 12582916
  214.1 7.5 %copy-start.2 = (bf16[2,16,4]{1,2,0:T(4,128)(2,1)S(1)}, bf16[2,16,4]{1,2,0:T(4,128)(2,1)}, u32[]{:S(2)}) copy-start(bf16[2,16,4]{1,2,0:T(4,128)(2,1)} %param.7) | copy-start | bytes 772
  214.1 103.6 %all-to-all-start.1 = ((bf16[4,4,128,4,2,128]{5,3,1,0,4,2:T(4,128)(2,1)}), bf16[4,4,128,4,2,128]{5,3,1,0,4,2:T(4,128)(2,1)}, u32[]{:S(2)}, u32[]{:S(2)}) async-start(bf16[4,4,128,4,2,128]{5,3,1,0,4,2:T(4,128)(2,1)} %copy.75), calls=%async_computation.1 | async-start | bytes 8388608 | tf_op jit(solution)/shard_map/all_to_all | solution.py:84
  221.5 187.5 %reduce-scatter.2.cloned.1.call-start = ((), (), s32[]{:S(2)}) async-start(), calls=%async_computation.4 | async-start | bytes 4718592 | tf_op jit(solution)/shard_map/reduce_scatter | solution.py:97
Sparse Core Ops, SparseCore 0:
  9.1 58.9 all-gather.1
  357.2 51.7 reduce-scatter.1
where the time goes:
time: 419 us; the launch traced here: 418 us
  waiting for transfers between devices  298 us (71%)
  local copies, waits for them, and re-layouts  32.4 us (8%)
  matrix products  29.8 us (7%)
  other arithmetic  27.2 us (6%)
  starting transfers between devices  17.7 us (4%)
  between operations  13.6 us (3%)
    all_to_all x1, waiting for transfers between devices, shards(): lax.all_to_all(row_pass, 'space', split_axis=3, concat_axis=2, tiled=True)  96.1 us
    all_to_all x1, waiting for transfers between devices, shards(): lax.all_to_all(back_first, 'space', split_axis=2, concat_axis=3, tiled=True)  96.1 us
    all_gather x1, waiting for transfers between devices, shards(): lax.all_gather(spatial_coef, 'coil', axis=0, tiled=True)  53.7 us
    reduce_scatter x1, waiting for transfers between devices, shards(): lax.psum_scatter(jnp.einsum('txypz,tplq->lxyqz', combined, adjoint_mix(se...  51.9 us
    dot_general x4, matrix products, transform(): return jnp.einsum(form, volume, table, preferred_element_type=jnp.float32)  17.2 us
    all_to_all x1, starting transfers between devices, shards(): lax.all_to_all(row_pass, 'space', split_axis=3, concat_axis=2, tiled=True)  10.2 us
    add x1, other arithmetic, shards(): combined_real = cosine * sum_real + sine * sum_imaginary  9.64 us
  transfers between devices with their start and end apart: 4, of which 4 were waited for; matrix products, arithmetic and copies ran while one was open for 1% of the time, Pallas kernels for 0%

commit v1 on v0

--- a/solution.py
+++ b/solution.py
@@ -49,9 +49,18 @@
 def shards(spatial_coef, temporal_basis, coil_maps, field_steps, kspace_data, sample_mask):
     points = temporal_basis.shape[2]
     section = temporal_basis
+    apply_squares = lambda row_data, row_axis: jnp.concatenate(
+        lax.all_to_all(
+            jnp.stack([row_data for _ in range(lax.axis_size(row_axis))]),
+            row_axis,
+            split_axis=0,
+            concat_axis=0,
+        ),
+        0,
+    )
     image = jnp.einsum(
         "lxypz,lptq->txyqz",
-        lax.all_gather(spatial_coef, "coil", axis=0, tiled=True),
+        apply_squares(spatial_coef, "coil"),
         forward_mix(section),
         preferred_element_type=jnp.float32,
     )

time: 419 us -> 442 us (1.055)
  local copies, waits for them, and re-layouts: 32.4 us -> 42.7 us
  starting transfers between devices: 17.7 us -> 26 us
    all_gather x1 -> x0, waiting for transfers between devices: 53.7 us -> none  [shards(): lax.all_gather(spatial_coef, 'coil', axis=0, tiled=True)]
    all_to_all x0 -> x1, waiting for transfers between devices: none -> 44.4 us  [shards(): lax.all_to_all(jnp.stack([row_data for _ in range(lax.axis_size(row_axis)...]
    reduce_scatter x1, waiting for transfers between devices: 51.9 us -> 65.9 us  [shards(): lax.psum_scatter(jnp.einsum('txypz,tplq->lxyqz', combined, adjoint_mix(se...]
    all_to_all x0 -> x1, starting transfers between devices: none -> 6.34 us  [shards(): lax.all_to_all(jnp.stack([row_data for _ in range(lax.axis_size(row_axis)...]
    another operation x0 -> x1, local copies, waits for them, and re-layouts: none -> 5.76 us  [shards(): jnp.stack([row_data for _ in range(lax.axis_size(row_axis))])]
    all_to_all x0 -> x1, local copies, waits for them, and re-layouts: none -> 5.29 us  [shards(): lax.all_to_all(jnp.stack([row_data for _ in range(lax.axis_size(row_axis)...]
where the time goes in v1:
time: 442 us; the launch traced here: 438 us
  waiting for transfers between devices  302 us (68%)
  local copies, waits for them, and re-layouts  42.7 us (10%)
  other arithmetic  27.5 us (6%)
  starting transfers between devices  26 us (6%)
  matrix products  25.7 us (6%)
  between operations  13.9 us (3%)
    all_to_all x1, waiting for transfers between devices, shards(): lax.all_to_all(back_first, 'space', split_axis=2, concat_axis=3, tiled=True)  96.1 us
    all_to_all x1, waiting for transfers between devices, shards(): lax.all_to_all(row_pass, 'space', split_axis=3, concat_axis=2, tiled=True)  96 us
    reduce_scatter x1, waiting for transfers between devices, shards(): lax.psum_scatter(jnp.einsum('txypz,tplq->lxyqz', combined, adjoint_mix(se...  65.9 us
    all_to_all x1, waiting for transfers between devices, shards(): lax.all_to_all(jnp.stack([row_data for _ in range(lax.axis_size(row_axis)...  44.4 us
    dot_general x4, matrix products, transform(): return jnp.einsum(form, volume, table, preferred_element_type=jnp.float32)  17.2 us
    all_to_all x1, starting transfers between devices, shards(): lax.all_to_all(row_pass, 'space', split_axis=3, concat_axis=2, tiled=True)  12.3 us
    add x1, other arithmetic, shards(): combined_real = cosine * sum_real + sine * sum_imaginary  9.64 us
  transfers between devices with their start and end apart: 4, of which 4 were waited for; matrix products, arithmetic and copies ran while one was open for 1% of the time, Pallas kernels for 0%

profile of v1, /device:TPU:1, one launch (start us, length us, event | category | flops | bytes accessed | tf_op | source)
XLA Modules:
  0.0 438.0 jit_solution(8924631036186541403)
XLA Ops:
  6.5 1.9 copy.65
  8.4 5.8 %stack.170 = bf16[8,2,4,128,2,128]{5,1,4,3,2,0:T(2,128)(2,1)} broadcast(bf16[2,4,128,2,128]{4,0,3,2,1:T(2,128)(2,1)S(1)} %copy.65), dimensions={1,2,3,4,5} | broadcast | bytes 4718592 | tf_op jit(solution)/shard_map/stack | solution.py:54
  14.2 0.0 copy-start.4
  14.2 6.3 %all-to-all-start = ((bf16[8,2,4,128,2,128]{5,1,4,3,2,0:T(2,128)(2,1)}), bf16[8,2,4,128,2,128]{5,1,4,3,2,0:T(2,128)(2,1)}, u32[]{:S(2)}, u32[]{:S(2)}) async-start(bf16[8,2,4,128,2,128]{5,1,4,3,2,0:T(2,128)(2,1)} %stack.170), calls=%async_computation | async-start | bytes 8388608 | tf_op jit(solution)/shard_map/all_to_all | solution.py:53
  20.5 0.0 copy-done.4
  20.6 0.3 multiply_convert_fusion.2
  20.8 0.3 negate_convert_fusion
  21.1 0.3 multiply_convert_fusion
  21.4 0.7 fusion.47
  22.1 3.6 slice_convert_fusion.1
  25.7 44.4 %all-to-all-done = bf16[8,2,4,128,2,128]{5,1,4,3,2,0:T(2,128)(2,1)} async-done(((bf16[8,2,4,128,2,128]{5,1,4,3,2,0:T(2,128)(2,1)}), bf16[8,2,4,128,2,128]{5,1,4,3,2,0:T(2,128)(2,1)}, u32[]{:S(2)}, u32[]{:S(2)}) %all-to-all-start) | async-done | bytes 4194336 | tf_op jit(solution)/shard_map/all_to_all | solution.py:53
  70.1 5.3 %copy.66 = bf16[8,2,4,128,2,128]{5,1,0,4,3,2:T(2,128)(2,1)S(1)} copy(bf16[8,2,4,128,2,128]{5,1,4,3,2,0:T(2,128)(2,1)} %all-to-all-done) | data formatting | bytes 8388608 | tf_op jit(solution)/shard_map/all_to_all | solution.py:53
  75.4 0.0 copy-start.1
  75.4 0.7 convolution_bitcast_fusion
  76.2 0.3 copy.128
  76.4 0.0 copy-done.1
  76.4 5.0 %multiply_subtract_fusion = (f32[4,4,128,128]{3,2,1,0:T(8,128)S(1)}, f32[4,4,128,128]{3,2,1,0:T(8,128)S(1)}) fusion(f32[4,4,128,2,128]{4,2,1,0,3:T(8,128)S(1)} %bitcast.244, s32[4]{0:T(128)S(1)} %iota_add_fusion, s32[4,128,128]{2,1,0:T(8,128)S(1)} %copy-done.1), kind=kLoop, calls=%fused_computation.61 | loop fusion | flops 5242880 | bytes 4456464 | tf_op jit(solution)/shard_map/sub | solution.py:70
  81.4 0.0 copy-start.2
  81.4 0.0 copy-start.3
  81.4 3.1 subtract_convert_fusion
  84.6 0.0 copy-done.2
  84.6 0.0 copy-done.3
  84.6 6.7 %fusion.5 = bf16[4,4,4,128,2,128]{5,3,2,1,0,4:T(8,128)(2,1)} fusion(bf16[4,4,4,128,1,128]{5,3,4,2,1,0:T(8,128)(2,1)} %get-tuple-element.8, bf16[4,4,4,128,1,128]{5,3,4,2,1,0:T(8,128)(2,1)} %get-tuple-element.7, bf16[1,128,2,128]{3,1,0,2:T(8,128)(2,1)S(1)} %copy-done.2, bf16[1,128,2,128]{3,1,0,2:T(8,128)(2,1)S(1)} %copy-done.3), kind=kOutput, calls=%fused_computation.10 | convolution fusion | flops 2160590848 | bytes 8519680 | tf_op jit(solution)/shard_map/ctxypz,pyqk->ctxkqz/dot_general | solution.py:46
  91.3 7.4 %copy.69 = bf16[4,4,4,128,2,128]{5,2,1,0,4,3:T(4,128)(2,1)} copy(bf16[4,4,4,128,2,128]{5,3,2,1,0,4:T(8,128)(2,1)} %fusion.5) | data formatting | bytes 8388608 | tf_op jit(solution)/shard_map/convert_element_type | solution.py:82
  98.7 0.0 copy-start.5
  98.7 12.3 %all-to-all-start.1 = ((bf16[4,4,4,128,2,128]{5,2,1,0,4,3:T(4,128)(2,1)}), bf16[4,4,4,128,2,128]{5,2,1,0,4,3:T(4,128)(2,1)}, u32[]{:S(2)}, u32[]{:S(2)}) async-start(bf16[4,4,4,128,2,128]{5,2,1,0,4,3:T(4,128)(2,1)} %copy.69), calls=%async_computation.1 | async-start | bytes 8388608 | tf_op jit(solution)/shard_map/all_to_all | solution.py:85
  111.0 0.0 copy-done.5
  111.1 96.0 %all-to-all-done.1 = bf16[4,4,4,128,2,128]{5,2,1,0,4,3:T(4,128)(2,1)} async-done(((bf16[4,4,4,128,2,128]{5,2,1,0,4,3:T(4,128)(2,1)}), bf16[4,4,4,128,2,128]{5,2,1,0,4,3:T(4,128)(2,1)}, u32[]{:S(2)}, u32[]{:S(2)}) %all-to-all-start.1) | async-done | bytes 4194336 | tf_op jit(solution)/shard_map/all_to_all | solution.py:85
  207.0 0.0 copy-start
  207.0 4.7 %copy.70 = bf16[4,4,4,32,4,2,128]{6,2,3,5,4,1,0:T(4,128)(2,1)S(1)} copy(bf16[4,4,4,32,4,2,128]{6,2,1,0,5,4,3:T(4,128)(2,1)} %bitcast.52) | data formatting | bytes 8388608 | tf_op jit(solution)/shard_map/all_to_all | solution.py:85
  211.7 0.0 copy-done
  211.8 1.4 fusion.1
  213.1 1.3 fusion.6
  214.4 5.2 %copy.75 = bf16[4,4,128,4,2,128]{5,3,1,0,4,2:T(4,128)(2,1)} copy(bf16[4,4,128,4,2,128]{5,2,3,1,0,4:T(8,128)(2,1)S(1)} %fusion.6) | data formatting | bytes 8388608 | tf_op jit(solution)/shard_map/convert_element_type | solution.py:90
  219.7 7.3 %all-to-all-start.2 = ((bf16[4,4,128,4,2,128]{5,3,1,0,4,2:T(4,128)(2,1)}), bf16[4,4,128,4,2,128]{5,3,1,0,4,2:T(4,128)(2,1)}, u32[]{:S(2)}, u32[]{:S(2)}) async-start(bf16[4,4,128,4,2,128]{5,3,1,0,4,2:T(4,128)(2,1)} %copy.75), calls=%async_computation.2 | async-start | bytes 8388608 | tf_op jit(solution)/shard_map/all_to_all | solution.py:93
  226.9 0.0 reduce-scatter.2.cloned.1.call-start
  227.0 96.1 %all-to-all-done.2 = bf16[4,4,128,4,2,128]{5,3,1,0,4,2:T(4,128)(2,1)} async-done(((bf16[4,4,128,4,2,128]{5,3,1,0,4,2:T(4,128)(2,1)}), bf16[4,4,128,4,2,128]{5,3,1,0,4,2:T(4,128)(2,1)}, u32[]{:S(2)}, u32[]{:S(2)}) %all-to-all-start.2) | async-done | bytes 4194336 | tf_op jit(solution)/shard_map/all_to_all | solution.py:93
  323.1 6.5 %copy.76 = bf16[4,4,32,4,4,2,128]{6,4,2,5,3,1,0:T(4,128)(2,1)} copy(bf16[4,4,32,4,4,2,128]{6,4,1,0,5,3,2:T(4,128)(2,1)} %bitcast.63) | data formatting | bytes 8388608 | tf_op jit(solution)/shard_map/all_to_all | solution.py:93
  329.6 7.8 %fusion.17 = f32[4,4,4,128,2,128]{5,3,4,2,1,0:T(8,128)} fusion(bf16[4,4,4,128,2,128,1]{5,3,6,4,2,1,0:T(8,128)(2,1)} %bitcast.237, bf16[1,128,2,128]{3,1,2,0:T(8,128)(2,1)S(1)} %get-tuple-element.18, bf16[1,128,2,128]{3,1,2,0:T(8,128)(2,1)S(1)} %get-tuple-element.15), kind=kOutput, calls=%fused_computation.28 | convolution fusion | flops 2150105088 | bytes 12713984 | tf_op jit(solution)/shard_map/ctxypz,pzqk->ctxyqk/dot_general | solution.py:46
  337.4 4.6 %add_reduce_fusion = (f32[4,4,128,128]{3,2,1,0:T(8,128)S(1)}, f32[4,4,128,128]{3,2,1,0:T(8,128)S(1)}) fusion(f32[4,4,4,128,2,128]{5,3,4,2,1,0:T(8,128)} %fusion.17, f32[4,4,128,128]{3,2,1,0:T(8,128)S(1)} %bitcast.243, f32[4,4,128,128]{3,2,1,0:T(8,128)S(1)} %bitcast.241), kind=kLoop, calls=%fused_computation.25 | loop fusion | flops 7864320 | bytes 12582912 | tf_op jit(solution)/shard_map/reduce_sum | solution.py:100
  342.0 9.6 %fusion.34 = (f32[4,4,128,1,128]{4,0,3,2,1:T(4,128)S(1)}, f32[4,4,128,1,128]{4,0,3,2,1:T(4,128)S(1)}) fusion(f32[4,4,128,128]{3,2,1,0:T(8,128)S(1)} %get-tuple-element.6, f32[4,4,128,128]{3,2,1,0:T(8,128)S(1)} %get-tuple-element.5, s32[4]{0:T(128)S(1)} %iota_add_fusion, s32[4,128,128]{2,1,0:T(8,128)S(1)} %copy-done.1), kind=kLoop, calls=%fused_computation.55 | loop fusion | flops 5242880 | bytes 4456464 | tf_op jit(solution)/shard_map/add | solution.py:102
  351.6 7.8 %fusion.7 = bf16[16,4,128,2,128]{4,0,2,1,3:T(8,128)(2,1)S(1)} fusion(f32[4,4,128,1,128]{4,0,3,2,1:T(4,128)S(1)} %get-tuple-element.10, f32[4,4,128,1,128]{4,0,3,2,1:T(4,128)S(1)} %get-tuple-element.9, f32[4,1,16,2]{2,0,1,3:T(4,128)S(1)} %get-tuple-element.22, f32[4,1,16,2]{2,0,1,3:T(4,128)S(1)} %get-tuple-element.21), kind=kOutput, calls=%fused_computation.12 | convolution fusion | flops 203948288 | bytes 6292480 | tf_op jit(solution)/shard_map/txypz,tplq->lxyqz/dot_general | solution.py:107
  359.4 3.1 copy.82
  362.4 0.0 reduce-scatter.2.cloned.1.call-update
  362.5 65.9 %reduce-scatter.2.cloned.1.call-done = bf16[2,4,128,2,128]{4,2,3,1,0:T(8,128)(2,1)} async-done(((bf16[16,4,128,2,128]{4,2,3,1,0:T(8,128)(2,1)}), bf16[2,4,128,2,128]{4,2,3,1,0:T(8,128)(2,1)}) %reduce-scatter.2.cloned.1.call-update) | async-done | bytes 524304 | tf_op jit(solution)/shard_map/reduce_scatter | solution.py:106
  428.4 2.6 copy.83
  (9 shorter events, 0.0 us)
Async XLA Ops:
  14.2 6.4 %copy-start.4 = (bf16[2,16,4]{1,2,0:T(4,128)(2,1)S(1)}, bf16[2,16,4]{1,2,0:T(4,128)(2,1)}, u32[]{:S(2)}) copy-start(bf16[2,16,4]{1,2,0:T(4,128)(2,1)} %param.7) | copy-start | bytes 772
  14.2 56.0 %all-to-all-start = ((bf16[8,2,4,128,2,128]{5,1,4,3,2,0:T(2,128)(2,1)}), bf16[8,2,4,128,2,128]{5,1,4,3,2,0:T(2,128)(2,1)}, u32[]{:S(2)}, u32[]{:S(2)}) async-start(bf16[8,2,4,128,2,128]{5,1,4,3,2,0:T(2,128)(2,1)} %stack.170), calls=%async_computation | async-start | bytes 8388608 | tf_op jit(solution)/shard_map/all_to_all | solution.py:53
  75.4 1.0 copy-start.1
  81.4 3.2 copy-start.2
  81.4 3.1 copy-start.3
  98.7 12.3 %copy-start.5 = (s32[4,4,128]{2,1,0:T(4,128)S(1)}, s32[4,4,128]{2,1,0:T(4,128)}, u32[]{:S(2)}) copy-start(s32[4,4,128]{2,1,0:T(4,128)} %param.11) | copy-start | bytes 24580
  98.7 108.3 %all-to-all-start.1 = ((bf16[4,4,4,128,2,128]{5,2,1,0,4,3:T(4,128)(2,1)}), bf16[4,4,4,128,2,128]{5,2,1,0,4,3:T(4,128)(2,1)}, u32[]{:S(2)}, u32[]{:S(2)}) async-start(bf16[4,4,4,128,2,128]{5,2,1,0,4,3:T(4,128)(2,1)} %copy.69), calls=%async_computation.1 | async-start | bytes 8388608 | tf_op jit(solution)/shard_map/all_to_all | solution.py:85
  207.0 4.7 %copy-start = (bf16[4,4,128,4,2,128]{5,4,3,2,1,0:T(2,128)(2,1)S(1)}, bf16[4,4,128,4,2,128]{5,4,3,2,1,0:T(2,128)(2,1)}, u32[]{:S(2)}) copy-start(bf16[4,4,128,4,2,128]{5,4,3,2,1,0:T(2,128)(2,1)} %param.10) | copy-start | bytes 12582916
  219.7 103.4 %all-to-all-start.2 = ((bf16[4,4,128,4,2,128]{5,3,1,0,4,2:T(4,128)(2,1)}), bf16[4,4,128,4,2,128]{5,3,1,0,4,2:T(4,128)(2,1)}, u32[]{:S(2)}, u32[]{:S(2)}) async-start(bf16[4,4,128,4,2,128]{5,3,1,0,4,2:T(4,128)(2,1)} %copy.75), calls=%async_computation.2 | async-start | bytes 8388608 | tf_op jit(solution)/shard_map/all_to_all | solution.py:93
  226.9 201.5 %reduce-scatter.2.cloned.1.call-start = ((), (), s32[]{:S(2)}) async-start(), calls=%async_computation.4 | async-start | bytes 4718592 | tf_op jit(solution)/shard_map/reduce_scatter | solution.py:106
Sparse Core Ops, SparseCore 0:
  362.6 65.7 reduce-scatter.1
